TPU v7x, 32 devices: a whole 2x2x4 slice. The times are simulated.
32 devices in a mesh: tok: 16 (over z, x, core), head: 2 (over y).
Axes of the slice: x: 2, y: 2, z: 4, core: 2. Of those that a mesh axis runs over, the one named last changes fastest.
Arguments:
- qkv: bfloat16 [2048, 3, 7168], P(('tok', 'head')), may hold values from -80 to 80
- prefix_cache: bfloat16 [16, 256, 2, 7168], P('tok', None, None, 'head'), may hold values from -80 to 80
- suffix_lengths: int32 [16, 8], P('tok'), may hold values from 1 to 24, 128 in all within a row
- request_groups: int32 [16, 8], P('tok'), may hold values from 0 to 15, all different within a row
- prefix_owner: int32 [16], replicated, may hold values from 0 to 15, each once
Outputs:
- attended: bfloat16 [2048, 7168], P(('tok', 'head'))
- suffix_cache: bfloat16 [2048, 2, 7168], P('tok', None, 'head')
Inputs may be any that keep to these rules, and one draw needn't show every extreme that they name: `suffix_lengths`: each row sums to 128; in each row the longest request has exactly 24 tokens. `request_groups`: the 8 requests of one row belong to 8 different groups; every group is read by some request. `prefix_owner`: every slot holds exactly one group.
All inputs are finite; a program needn't handle non-finite values.
Results may differ from a plain program's by a relative error of at most 0.003.
Values may be sent and summed in bfloat16 or wider, within the bound.
A program may use at most 64 MiB of HBM per device.

v0:
```python
import math
import jax
import jax.numpy as jnp
from jax import lax
from jax.sharding import PartitionSpec as P

HD = 224


def prefix_partials(received, cache_keys, cache_values, scale):
    sources, items, width = received.shape
    heads = cache_keys.shape[1]
    query = received.reshape(sources * items, heads, width // heads)
    scores = (
        jnp.einsum("rhd,phd->hrp", query, cache_keys, preferred_element_type=jnp.float32) * scale
    )
    peak = jnp.max(scores, axis=2)
    raised = jnp.exp(scores - peak[:, :, None])
    total = jnp.sum(raised, axis=2)
    mixed = jnp.einsum(
        "hrp,phd->rhd",
        raised.astype(jnp.bfloat16),
        cache_values,
        preferred_element_type=jnp.float32,
    )
    mixed = mixed / jnp.transpose(total)[:, :, None]
    mixed = mixed.reshape(sources, items, width)
    peak = jnp.transpose(peak).reshape(sources, items, heads)
    total = jnp.transpose(total).reshape(sources, items, heads)
    return (mixed, peak, total)


def send_back(mixed, peak, total):
    return (
        lax.all_to_all(mixed, "tok", split_axis=0, concat_axis=0, tiled=True),
        lax.all_to_all(peak, "tok", split_axis=0, concat_axis=0, tiled=True),
        lax.all_to_all(total, "tok", split_axis=0, concat_axis=0, tiled=True),
    )


def per_device(qkv, prefix_cache, suffix_lengths, request_groups, prefix_owner):
    regrouped = lax.all_to_all(qkv, "head", split_axis=2, concat_axis=0, tiled=True)
    tok_rows = regrouped.shape[0]
    width = regrouped.shape[2]
    head_dim = HD
    heads = width // head_dim
    scale = 1.0 / math.sqrt(head_dim)
    query = regrouped[:, 0].reshape(tok_rows, heads, head_dim)
    keyrows = regrouped[:, 1].reshape(tok_rows, heads, head_dim)
    values = regrouped[:, 2].reshape(tok_rows, heads, head_dim)
    lengths = suffix_lengths[0]
    groups = request_groups[0]
    requests = lengths.shape[0]
    ends = jnp.cumsum(lengths)
    starts = ends - lengths
    position = jnp.arange(tok_rows, dtype=jnp.int32)
    request = jnp.sum((position[:, None] >= ends[None, :]).astype(jnp.int32), axis=1)
    scores = jnp.einsum("thd,shd->hts", query, keyrows, preferred_element_type=jnp.float32) * scale
    allowed = (request[:, None] == request[None, :]) & (position[None, :] <= position[:, None])
    scores = jnp.where(allowed[None], scores, -jnp.inf)
    peak_s = jnp.max(scores, axis=2)
    raised = jnp.exp(scores - peak_s[:, :, None])
    total_s = jnp.sum(raised, axis=2)
    mixed_s = jnp.einsum(
        "hts,shd->thd", raised.astype(jnp.bfloat16), values, preferred_element_type=jnp.float32
    )
    request_onehot = (request[:, None] == jnp.arange(requests, dtype=jnp.int32)[None, :]).astype(
        jnp.int32
    )
    token_group = jnp.sum(request_onehot * groups[None, :], axis=1)
    token_start = jnp.sum(request_onehot * starts[None, :], axis=1)
    offset = position - token_start
    owners = prefix_owner.shape[0]
    group_onehot = (token_group[:, None] == jnp.arange(owners, dtype=jnp.int32)[None, :]).astype(
        jnp.int32
    )
    slot = jnp.sum(group_onehot * prefix_owner[None, :], axis=1)
    capacity = 3 * tok_rows // lax.axis_size("tok")
    outgoing = (
        jnp.zeros((owners, capacity, width), jnp.bfloat16).at[slot, offset].set(regrouped[:, 0])
    )
    prefix_len = prefix_cache.shape[1]
    cache_keys = prefix_cache[0, :, 0].reshape(prefix_len, heads, head_dim)
    cache_values = prefix_cache[0, :, 1].reshape(prefix_len, heads, head_dim)
    received = lax.all_to_all(outgoing, "tok", split_axis=0, concat_axis=0, tiled=True)
    mixed, peak, total = prefix_partials(received, cache_keys, cache_values, scale)
    mixed_back, peak_back, total_back = send_back(mixed, peak, total)
    o_tok = mixed_back[slot, offset].reshape(tok_rows, heads, head_dim)
    m_tok = peak_back[slot, offset]
    l_tok = total_back[slot, offset]
    m_s = jnp.transpose(peak_s)
    l_s = jnp.transpose(total_s)
    top = jnp.maximum(m_tok, m_s)
    first = l_tok * jnp.exp(m_tok - top)
    second = jnp.exp(m_s - top)
    merged = (first[:, :, None] * o_tok + second[:, :, None] * mixed_s) / (first + second * l_s)[
        :, :, None
    ]
    merged = merged.reshape(tok_rows, width).astype(jnp.bfloat16)
    attended = lax.all_to_all(merged, "head", split_axis=0, concat_axis=1, tiled=True)
    suffix_cache = regrouped[:, 1:3]
    return (attended, suffix_cache)


def solution(mesh):
    in_specs = (
        P(("tok", "head"), None, None),
        P("tok", None, None, "head"),
        P("tok", None),
        P("tok", None),
        P(),
    )
    out_specs = (P(("tok", "head"), None), P("tok", None, "head"))
    return jax.shard_map(
        per_device, mesh=mesh, in_specs=in_specs, out_specs=out_specs, check_vma=False
    )
```

profile of v0, /device:TPU:10, one launch (start us, length us, event | category | flops | bytes accessed | tf_op | source)
XLA Modules:
  0.0 395.5 jit_solution(12547379650394092253)
XLA Ops:
  0.6 10.0 %copy.133 = bf16[64,3,7168]{0,1,2:T(4,128)(2,1)} copy(bf16[64,3,7168]{2,0,1:T(8,128)(2,1)} %param.5) | data formatting | bytes 5505024 | tf_op args[0]
  10.7 8.1 %reshape.146 = bf16[2,2,344064]{2,1,0:T(2,128)(2,1)} reshape(bf16[7168,3,64]{2,1,0:T(4,128)(2,1)} %bitcast.92) | data formatting | bytes 5505024
  18.7 4.0 %all-to-all-start = ((bf16[2,2,344064]{2,1,0:T(2,128)(2,1)}), bf16[2,2,344064]{2,1,0:T(2,128)(2,1)S(1)}, u32[]{:S(2)}, u32[]{:S(2)}) async-start(bf16[2,2,344064]{2,1,0:T(2,128)(2,1)} %reshape.146), calls=%async_computation | async-start | bytes 5505024 | tf_op jit(solution)/shard_map/all_to_all | solution.py:42
  22.8 0.2 reduce-window.4
  23.3 31.6 %all-to-all-done = bf16[2,2,344064]{2,1,0:T(2,128)(2,1)S(1)} async-done(((bf16[2,2,344064]{2,1,0:T(2,128)(2,1)}), bf16[2,2,344064]{2,1,0:T(2,128)(2,1)S(1)}, u32[]{:S(2)}, u32[]{:S(2)}) %all-to-all-start) | async-done | bytes 2752544 | tf_op jit(solution)/shard_map/all_to_all | solution.py:42
  54.9 6.1 %reshape.147 = bf16[7168,3,64]{2,1,0:T(4,128)(2,1)} reshape(bf16[2,2,344064]{2,1,0:T(2,128)(2,1)S(1)} %all-to-all-done) | data formatting | bytes 5505024
  61.0 8.9 %copy.134 = bf16[64,3,2,3584]{3,0,2,1:T(8,128)(2,1)S(1)} copy(bf16[64,3,2,3584]{0,1,3,2:T(4,128)(2,1)} %bitcast.91) | data formatting | bytes 5505024 | tf_op jit(solution)/shard_map/all_to_all | solution.py:42
  69.8 2.0 fusion.31
  71.8 1.7 broadcast_in_dim.10
  73.5 33.3 %scatter_fusion = bf16[16,24,3584]{2,1,0:T(8,128)(2,1)} fusion(bf16[16,24,3584]{2,1,0:T(8,128)(2,1)} %broadcast_in_dim.10, s32[128]{0:T(128)S(1)} %get-tuple-element.26, bf16[128,3584]{1,0:T(8,128)(2,1)} %get-tuple-element.22), kind=kCustom, calls=%fused_computation.3 | custom fusion | bytes 2753536 | tf_op jit(solution)/shard_map/scatter | solution.py:80
  106.9 6.4 %all-to-all-start.1 = ((bf16[16,24,3584]{2,1,0:T(8,128)(2,1)}), bf16[16,24,3584]{2,1,0:T(8,128)(2,1)}, u32[]{:S(2)}, u32[]{:S(2)}) async-start(bf16[16,24,3584]{2,1,0:T(8,128)(2,1)} %scatter_fusion), calls=%async_computation.1 | async-start | bytes 5505024 | tf_op jit(solution)/shard_map/all_to_all | solution.py:85
  113.3 8.7 %fusion.30 = (bf16[1,256,1,3584]{3,2,1,0:T(2,128)(2,1)}, bf16[1,256,1,3584]{3,2,1,0:T(2,128)(2,1)}) fusion(bf16[1,256,2,3584]{3,2,1,0:T(2,128)(2,1)} %param.6), kind=kLoop, calls=%fused_computation.53 | loop fusion | bytes 7340032 | tf_op jit(solution)/shard_map/slice | solution.py:84
  122.0 8.5 %copy.135 = bf16[1,256,1,3584]{1,3,2,0:T(8,128)(2,1)} copy(bf16[1,256,1,3584]{3,2,1,0:T(2,128)(2,1)} %get-tuple-element.20) | data formatting | bytes 3670016 | tf_op jit(solution)/shard_map/slice | solution.py:83
  130.5 44.1 %all-to-all-done.1 = bf16[16,24,3584]{2,1,0:T(8,128)(2,1)} async-done(((bf16[16,24,3584]{2,1,0:T(8,128)(2,1)}), bf16[16,24,3584]{2,1,0:T(8,128)(2,1)}, u32[]{:S(2)}, u32[]{:S(2)}) %all-to-all-start.1) | async-done | bytes 2752544 | tf_op jit(solution)/shard_map/all_to_all | solution.py:85
  174.6 7.2 %reshape.117 = bf16[384,16,224]{2,1,0:T(8,128)(2,1)} reshape(bf16[16,24,3584]{2,1,0:T(8,128)(2,1)} %all-to-all-done.1) | data formatting | bytes 5505024 | tf_op jit(solution)/shard_map/reshape | solution.py:13
  181.8 5.2 %multiply_reduce_fusion = (f32[16,384]{1,0:T(8,128)S(1)}, f32[16,384,256]{1,2,0:T(8,128)S(1)}) fusion(bf16[256,16,224]{0,2,1:T(8,128)(2,1)} %bitcast.95, bf16[384,16,224]{2,1,0:T(8,128)(2,1)} %reshape.117), kind=kOutput, calls=%fused_computation.5 | convolution fusion | flops 707782656 | bytes 10903552 | tf_op jit(solution)/shard_map/rhd,phd->hrp/dot_general | solution.py:15
  187.0 1.1 fusion.1
  188.1 1.6 copy-done
  189.9 0.7 reshape.148
  190.6 5.1 %all-to-all-start.2 = ((f32[16,1,384]{2,1,0:T(1,128)}), f32[16,1,384]{2,1,0:T(1,128)S(1)}, u32[]{:S(2)}, u32[]{:S(2)}) async-start(f32[16,1,384]{2,1,0:T(1,128)} %reshape.148), calls=%async_computation.2 | async-start | bytes 49152 | tf_op jit(solution)/shard_map/all_to_all | solution.py:37
  195.7 8.5 %copy.146 = bf16[1,256,1,3584]{1,3,2,0:T(8,128)(2,1)} copy(bf16[1,256,1,3584]{3,2,1,0:T(2,128)(2,1)} %get-tuple-element.19) | data formatting | bytes 3670016 | tf_op jit(solution)/shard_map/slice | solution.py:84
  204.4 0.7 reshape.150
  205.1 6.0 %all-to-all-start.3 = ((f32[16,1,384]{2,1,0:T(1,128)}), f32[16,1,384]{2,1,0:T(1,128)S(1)}, u32[]{:S(2)}, u32[]{:S(2)}) async-start(f32[16,1,384]{2,1,0:T(1,128)} %reshape.150), calls=%async_computation.3 | async-start | bytes 49152 | tf_op jit(solution)/shard_map/all_to_all | solution.py:36
  211.1 7.2 %bitcast_divide_fusion = f32[384,16,224]{0,2,1:T(8,128)} fusion(f32[384,16]{0,1:T(8,128)S(1)} %bitcast.108, bf16[256,16,224]{0,2,1:T(8,128)(2,1)} %bitcast.99, f32[16,384,256]{1,2,0:T(8,128)} %copy-done, f32[16,384]{1,0:T(8,128)S(1)} %get-tuple-element.27), kind=kOutput, calls=%fused_computation.6 | convolution fusion | flops 710737920 | bytes 13680640 | tf_op jit(solution)/shard_map/hrp,phd->rhd/dot_general | solution.py:20
  218.3 6.7 %copy.148 = f32[384,16,224]{2,1,0:T(8,128)} copy(f32[384,16,224]{0,2,1:T(8,128)} %bitcast_divide_fusion) | data formatting | bytes 11010048 | tf_op jit(solution)/shard_map/div | solution.py:26
  224.9 7.9 %reshape.120 = f32[16,24,3584]{2,1,0:T(8,128)} reshape(f32[384,16,224]{2,1,0:T(8,128)} %copy.148) | data formatting | bytes 11010048 | tf_op jit(solution)/shard_map/reshape | solution.py:27
  232.8 6.0 %all-to-all-start.4 = ((f32[16,24,3584]{2,1,0:T(8,128)}), f32[16,24,3584]{2,1,0:T(8,128)}, u32[]{:S(2)}, u32[]{:S(2)}) async-start(f32[16,24,3584]{2,1,0:T(8,128)} %reshape.120), calls=%async_computation.4 | async-start | bytes 11010048 | tf_op jit(solution)/shard_map/all_to_all | solution.py:35
  238.9 2.2 copy.142
  241.2 2.2 copy.150
  243.4 2.2 copy.141
  245.6 2.0 fusion.32
  247.6 1.0 copy-done.1
  248.6 0.2 fusion.14
  248.7 0.5 broadcast.192
  249.2 0.7 reduce.1
  250.2 1.2 gather_fusion
  251.5 0.7 reduce
  252.4 1.2 gather_fusion.1
  253.7 105.4 %all-to-all-done.4 = f32[16,24,3584]{2,1,0:T(8,128)} async-done(((f32[16,24,3584]{2,1,0:T(8,128)}), f32[16,24,3584]{2,1,0:T(8,128)}, u32[]{:S(2)}, u32[]{:S(2)}) %all-to-all-start.4) | async-done | bytes 5505056 | tf_op jit(solution)/shard_map/all_to_all | solution.py:35
  359.1 4.5 %gather_fusion.2 = f32[128,3584]{1,0:T(8,128)} fusion(f32[16,24,3584]{2,1,0:T(8,128)} %all-to-all-done.4, s32[128]{0:T(128)S(1)} %get-tuple-element.25), kind=kCustom, calls=%fused_computation.2 | custom fusion | bytes 3671040 | tf_op jit(solution)/shard_map/gather | solution.py:88
  363.6 2.7 copy.149
  366.4 3.6 fusion.10
  370.0 2.6 copy.152
  372.6 3.3 convert_element_type.22
  375.9 4.4 %all-to-all-start.5 = ((bf16[2,64,3584]{2,1,0:T(8,128)(2,1)}), bf16[2,64,3584]{2,1,0:T(8,128)(2,1)}, u32[]{:S(2)}, u32[]{:S(2)}) async-start(bf16[2,64,3584]{2,1,0:T(8,128)(2,1)} %convert_element_type.22), calls=%async_computation.5 | async-start | bytes 1835008 | tf_op jit(solution)/shard_map/all_to_all | solution.py:100
  380.4 3.1 copy.154
  383.5 9.9 %all-to-all-done.5 = bf16[2,64,3584]{2,1,0:T(8,128)(2,1)} async-done(((bf16[2,64,3584]{2,1,0:T(8,128)(2,1)}), bf16[2,64,3584]{2,1,0:T(8,128)(2,1)}, u32[]{:S(2)}, u32[]{:S(2)}) %all-to-all-start.5) | async-done | bytes 917536 | tf_op jit(solution)/shard_map/all_to_all | solution.py:100
  393.4 2.2 copy.157
  (28 shorter events, 1.3 us)
Async XLA Ops:
  18.7 4.0 %copy-start.3 = (s32[1,8]{1,0:T(1,128)S(1)}, s32[1,8]{1,0:T(1,128)}, u32[]{:S(2)}) copy-start(s32[1,8]{1,0:T(1,128)} %param.7) | copy-start | bytes 100
  18.7 4.3 %copy-start.2 = (s32[1,8]{1,0:T(1,128)S(1)}, s32[1,8]{1,0:T(1,128)}, u32[]{:S(2)}) copy-start(s32[1,8]{1,0:T(1,128)} %param.8) | copy-start | bytes 100
  18.7 4.4 %copy-start.4 = (s32[16]{0:T(128)S(1)}, s32[16]{0:T(128)}, u32[]{:S(2)}) copy-start(s32[16]{0:T(128)} %param.9) | copy-start | bytes 196
  18.7 36.1 %all-to-all-start = ((bf16[2,2,344064]{2,1,0:T(2,128)(2,1)}), bf16[2,2,344064]{2,1,0:T(2,128)(2,1)S(1)}, u32[]{:S(2)}, u32[]{:S(2)}) async-start(bf16[2,2,344064]{2,1,0:T(2,128)(2,1)} %reshape.146), calls=%async_computation | async-start | bytes 5505024 | tf_op jit(solution)/shard_map/all_to_all | solution.py:42
  106.9 67.7 %all-to-all-start.1 = ((bf16[16,24,3584]{2,1,0:T(8,128)(2,1)}), bf16[16,24,3584]{2,1,0:T(8,128)(2,1)}, u32[]{:S(2)}, u32[]{:S(2)}) async-start(bf16[16,24,3584]{2,1,0:T(8,128)(2,1)} %scatter_fusion), calls=%async_computation.1 | async-start | bytes 5505024 | tf_op jit(solution)/shard_map/all_to_all | solution.py:85
  187.0 2.7 copy-start
  190.6 14.5 %all-to-all-start.2 = ((f32[16,1,384]{2,1,0:T(1,128)}), f32[16,1,384]{2,1,0:T(1,128)S(1)}, u32[]{:S(2)}, u32[]{:S(2)}) async-start(f32[16,1,384]{2,1,0:T(1,128)} %reshape.148), calls=%async_computation.2 | async-start | bytes 49152 | tf_op jit(solution)/shard_map/all_to_all | solution.py:37
  205.1 27.7 %all-to-all-start.3 = ((f32[16,1,384]{2,1,0:T(1,128)}), f32[16,1,384]{2,1,0:T(1,128)S(1)}, u32[]{:S(2)}, u32[]{:S(2)}) async-start(f32[16,1,384]{2,1,0:T(1,128)} %reshape.150), calls=%async_computation.3 | async-start | bytes 49152 | tf_op jit(solution)/shard_map/all_to_all | solution.py:36
  232.8 126.3 %all-to-all-start.4 = ((f32[16,24,3584]{2,1,0:T(8,128)}), f32[16,24,3584]{2,1,0:T(8,128)}, u32[]{:S(2)}, u32[]{:S(2)}) async-start(f32[16,24,3584]{2,1,0:T(8,128)} %reshape.120), calls=%async_computation.4 | async-start | bytes 11010048 | tf_op jit(solution)/shard_map/all_to_all | solution.py:35
  247.6 1.0 copy-start.1
  375.9 17.5 %all-to-all-start.5 = ((bf16[2,64,3584]{2,1,0:T(8,128)(2,1)}), bf16[2,64,3584]{2,1,0:T(8,128)(2,1)}, u32[]{:S(2)}, u32[]{:S(2)}) async-start(bf16[2,64,3584]{2,1,0:T(8,128)(2,1)} %convert_element_type.22), calls=%async_computation.5 | async-start | bytes 1835008 | tf_op jit(solution)/shard_map/all_to_all | solution.py:100
where the time goes:
time: 398 us; the launch traced here: 396 us
  waiting for transfers between devices  191 us (48%)
  local copies, waits for them, and re-layouts  151 us (38%)
  starting transfers between devices  31.9 us (8%)
  matrix products  17.9 us (4%)
    all_to_all x1, waiting for transfers between devices, send_back(): lax.all_to_all(mixed, 'tok', split_axis=0, concat_axis=0, tiled=True)  105 us
    all_to_all x1, waiting for transfers between devices, per_device(): lax.all_to_all(outgoing, 'tok', split_axis=0, concat_axis=0, tiled=True)  44.1 us
    scatter x1, local copies, waits for them, and re-layouts, per_device(): jnp.zeros((owners, capacity, width), jnp.bfloat16).at[slot, offset]  33.3 us
    all_to_all x1, waiting for transfers between devices, per_device(): lax.all_to_all(qkv, 'head', split_axis=2, concat_axis=0, tiled=True)  31.6 us
    unnamed x18, local copies, waits for them, and re-layouts  31.5 us
    slice x2, local copies, waits for them, and re-layouts, per_device(): cache_values = prefix_cache[0, :, 1].reshape(prefix_len, heads, head_dim)  17.2 us
    all_to_all x1, waiting for transfers between devices, per_device(): lax.all_to_all(merged, 'head', split_axis=0, concat_axis=1, tiled=True)  9.87 us
    all_to_all x1, local copies, waits for them, and re-layouts, per_device(): lax.all_to_all(qkv, 'head', split_axis=2, concat_axis=0, tiled=True)  8.86 us
  transfers between devices with their start and end apart: 6, of which 4 were waited for; matrix products, arithmetic and copies ran while one was open for 17% of the time, Pallas kernels for 0%

commit v1 on v0

--- a/solution.py
+++ b/solution.py
@@ -3,6 +3,7 @@
 import jax.numpy as jnp
 from jax import lax
 from jax.sharding import PartitionSpec as P
+from jax.lax import all_to_all, axis_size
 
 HD = 224
 
@@ -39,7 +40,16 @@
 
 
 def per_device(qkv, prefix_cache, suffix_lengths, request_groups, prefix_owner):
-    regrouped = lax.all_to_all(qkv, "head", split_axis=2, concat_axis=0, tiled=True)
+    object_clear = lambda q_in, lane_axis: jnp.concatenate(
+        all_to_all(
+            jnp.stack(jnp.split(q_in, axis_size(lane_axis), axis=2)),
+            axis_name=lane_axis,
+            split_axis=0,
+            concat_axis=0,
+        ),
+        axis=0,
+    )
+    regrouped = object_clear(qkv, "head")
     tok_rows = regrouped.shape[0]
     width = regrouped.shape[2]
     head_dim = HD

time: 398 us -> 371 us (0.932)
  local copies, waits for them, and re-layouts: 151 us -> 121 us
    unnamed x18 -> x15, local copies, waits for them, and re-layouts: 31.5 us -> 7.35 us
    all_to_all x1, local copies, waits for them, and re-layouts: 8.86 us -> 1.95 us  [per_device(): all_to_all(jnp.stack(jnp.split(q_in, axis_size(lane_axis), axis=2)), axis...]
  transfers between devices with their start and end apart: 6 -> 6, of which waited for: 4 -> 4; matrix products, arithmetic and copies ran while one was open for 17% -> 18% of each run, Pallas kernels for 0% -> 0%
where the time goes in v1:
time: 371 us; the launch traced here: 369 us
  waiting for transfers between devices  191 us (51%)
  local copies, waits for them, and re-layouts  121 us (33%)
  starting transfers between devices  33.1 us (9%)
  matrix products  17.9 us (5%)
  other arithmetic  5.07 us (1%)
    all_to_all x1, waiting for transfers between devices, send_back(): lax.all_to_all(mixed, 'tok', split_axis=0, concat_axis=0, tiled=True)  105 us
    all_to_all x1, waiting for transfers between devices, per_device(): lax.all_to_all(outgoing, 'tok', split_axis=0, concat_axis=0, tiled=True)  44.1 us
    scatter x1, local copies, waits for them, and re-layouts, per_device(): jnp.zeros((owners, capacity, width), jnp.bfloat16).at[slot, offset]  33.3 us
    all_to_all x1, waiting for transfers between devices, per_device(): all_to_all(jnp.stack(jnp.split(q_in, axis_size(lane_axis), axis=2)), axis...  31.7 us
    slice x2, local copies, waits for them, and re-layouts, per_device(): cache_values = prefix_cache[0, :, 1].reshape(prefix_len, heads, head_dim)  17.2 us
    all_to_all x1, waiting for transfers between devices, per_device(): lax.all_to_all(merged, 'head', split_axis=0, concat_axis=1, tiled=True)  9.88 us
    slice x1, local copies, waits for them, and re-layouts, per_device(): cache_keys = prefix_cache[0, :, 0].reshape(prefix_len, heads, head_dim)  8.53 us
    reshape x1, local copies, waits for them, and re-layouts, prefix_partials(): mixed = mixed.reshape(sources, items, width)  7.89 us
  transfers between devices with their start and end apart: 6, of which 4 were waited for; matrix products, arithmetic and copies ran while one was open for 18% of the time, Pallas kernels for 0%

profile of v1, /device:TPU:10, one launch (start us, length us, event | category | flops | bytes accessed | tf_op | source)
XLA Modules:
  0.0 369.5 jit_solution(2154363506061868609)
XLA Ops:
  0.6 1.9 slice_bitcast_fusion.1
  2.6 1.8 pad_maximum_fusion
  4.4 5.2 %all-to-all-start = ((bf16[2,64,3,3584]{3,1,2,0:T(8,128)(2,1)}), bf16[2,64,3,3584]{3,1,2,0:T(8,128)(2,1)}, u32[]{:S(2)}, u32[]{:S(2)}) async-start(bf16[2,64,3,3584]{3,1,2,0:T(8,128)(2,1)} %pad_maximum_fusion), calls=%async_computation | async-start | bytes 5505024 | tf_op jit(solution)/shard_map/all_to_all | solution.py:44
  9.6 0.2 reduce-window.4
  10.0 31.7 %all-to-all-done = bf16[2,64,3,3584]{3,1,2,0:T(8,128)(2,1)} async-done(((bf16[2,64,3,3584]{3,1,2,0:T(8,128)(2,1)}), bf16[2,64,3,3584]{3,1,2,0:T(8,128)(2,1)}, u32[]{:S(2)}, u32[]{:S(2)}) %all-to-all-start) | async-done | bytes 2752544 | tf_op jit(solution)/shard_map/all_to_all | solution.py:44
  41.8 2.0 copy.130
  43.7 2.0 fusion.31
  45.7 1.7 broadcast_in_dim.10
  47.4 33.3 %scatter_fusion = bf16[16,24,3584]{2,1,0:T(8,128)(2,1)} fusion(bf16[16,24,3584]{2,1,0:T(8,128)(2,1)} %broadcast_in_dim.10, s32[128]{0:T(128)S(1)} %get-tuple-element.28, bf16[128,3584]{1,0:T(8,128)(2,1)} %get-tuple-element.22), kind=kCustom, calls=%fused_computation.3 | custom fusion | bytes 2753536 | tf_op jit(solution)/shard_map/scatter | solution.py:90
  80.8 6.4 %all-to-all-start.1 = ((bf16[16,24,3584]{2,1,0:T(8,128)(2,1)}), bf16[16,24,3584]{2,1,0:T(8,128)(2,1)}, u32[]{:S(2)}, u32[]{:S(2)}) async-start(bf16[16,24,3584]{2,1,0:T(8,128)(2,1)} %scatter_fusion), calls=%async_computation.1 | async-start | bytes 5505024 | tf_op jit(solution)/shard_map/all_to_all | solution.py:95
  87.2 8.7 %fusion.30 = (bf16[1,256,1,3584]{3,2,1,0:T(2,128)(2,1)}, bf16[1,256,1,3584]{3,2,1,0:T(2,128)(2,1)}) fusion(bf16[1,256,2,3584]{3,2,1,0:T(2,128)(2,1)} %param.6), kind=kLoop, calls=%fused_computation.56 | loop fusion | bytes 7340032 | tf_op jit(solution)/shard_map/slice | solution.py:94
  95.9 8.5 %copy.131 = bf16[1,256,1,3584]{1,3,2,0:T(8,128)(2,1)} copy(bf16[1,256,1,3584]{3,2,1,0:T(2,128)(2,1)} %get-tuple-element.20) | data formatting | bytes 3670016 | tf_op jit(solution)/shard_map/slice | solution.py:93
  104.4 44.1 %all-to-all-done.1 = bf16[16,24,3584]{2,1,0:T(8,128)(2,1)} async-done(((bf16[16,24,3584]{2,1,0:T(8,128)(2,1)}), bf16[16,24,3584]{2,1,0:T(8,128)(2,1)}, u32[]{:S(2)}, u32[]{:S(2)}) %all-to-all-start.1) | async-done | bytes 2752544 | tf_op jit(solution)/shard_map/all_to_all | solution.py:95
  148.5 7.2 %reshape.121 = bf16[384,16,224]{2,1,0:T(8,128)(2,1)} reshape(bf16[16,24,3584]{2,1,0:T(8,128)(2,1)} %all-to-all-done.1) | data formatting | bytes 5505024 | tf_op jit(solution)/shard_map/reshape | solution.py:14
  155.7 5.2 %multiply_reduce_fusion = (f32[16,384]{1,0:T(8,128)S(1)}, f32[16,384,256]{1,2,0:T(8,128)S(1)}) fusion(bf16[256,16,224]{0,2,1:T(8,128)(2,1)} %bitcast.92, bf16[384,16,224]{2,1,0:T(8,128)(2,1)} %reshape.121), kind=kOutput, calls=%fused_computation.5 | convolution fusion | flops 707782656 | bytes 10903552 | tf_op jit(solution)/shard_map/rhd,phd->hrp/dot_general | solution.py:16
  160.9 1.1 fusion.1
  162.0 1.6 copy-done
  163.8 0.7 reshape.150
  164.5 5.1 %all-to-all-start.2 = ((f32[16,1,384]{2,1,0:T(1,128)}), f32[16,1,384]{2,1,0:T(1,128)S(1)}, u32[]{:S(2)}, u32[]{:S(2)}) async-start(f32[16,1,384]{2,1,0:T(1,128)} %reshape.150), calls=%async_computation.2 | async-start | bytes 49152 | tf_op jit(solution)/shard_map/all_to_all | solution.py:38
  169.6 8.5 %copy.142 = bf16[1,256,1,3584]{1,3,2,0:T(8,128)(2,1)} copy(bf16[1,256,1,3584]{3,2,1,0:T(2,128)(2,1)} %get-tuple-element.19) | data formatting | bytes 3670016 | tf_op jit(solution)/shard_map/slice | solution.py:94
  178.3 0.7 reshape.152
  179.0 6.0 %all-to-all-start.3 = ((f32[16,1,384]{2,1,0:T(1,128)}), f32[16,1,384]{2,1,0:T(1,128)S(1)}, u32[]{:S(2)}, u32[]{:S(2)}) async-start(f32[16,1,384]{2,1,0:T(1,128)} %reshape.152), calls=%async_computation.3 | async-start | bytes 49152 | tf_op jit(solution)/shard_map/all_to_all | solution.py:37
  185.0 7.2 %bitcast_divide_fusion = f32[384,16,224]{0,2,1:T(8,128)} fusion(f32[384,16]{0,1:T(8,128)S(1)} %bitcast.105, bf16[256,16,224]{0,2,1:T(8,128)(2,1)} %bitcast.96, f32[16,384,256]{1,2,0:T(8,128)} %copy-done, f32[16,384]{1,0:T(8,128)S(1)} %get-tuple-element.29), kind=kOutput, calls=%fused_computation.6 | convolution fusion | flops 710737920 | bytes 13680640 | tf_op jit(solution)/shard_map/hrp,phd->rhd/dot_general | solution.py:21
  192.2 6.7 %copy.144 = f32[384,16,224]{2,1,0:T(8,128)} copy(f32[384,16,224]{0,2,1:T(8,128)} %bitcast_divide_fusion) | data formatting | bytes 11010048 | tf_op jit(solution)/shard_map/div | solution.py:27
  198.9 7.9 %reshape.124 = f32[16,24,3584]{2,1,0:T(8,128)} reshape(f32[384,16,224]{2,1,0:T(8,128)} %copy.144) | data formatting | bytes 11010048 | tf_op jit(solution)/shard_map/reshape | solution.py:28
  206.7 6.0 %all-to-all-start.4 = ((f32[16,24,3584]{2,1,0:T(8,128)}), f32[16,24,3584]{2,1,0:T(8,128)}, u32[]{:S(2)}, u32[]{:S(2)}) async-start(f32[16,24,3584]{2,1,0:T(8,128)} %reshape.124), calls=%async_computation.4 | async-start | bytes 11010048 | tf_op jit(solution)/shard_map/all_to_all | solution.py:36
  212.9 2.2 copy.138
  215.1 2.2 copy.146
  217.3 2.2 copy.137
  219.5 2.0 fusion.32
  221.5 1.0 copy-done.1
  222.5 0.2 fusion.14
  222.6 0.5 broadcast.192
  223.2 0.7 reduce.1
  224.1 1.2 gather_fusion
  225.4 0.7 reduce
  226.3 1.2 gather_fusion.1
  227.7 105.4 %all-to-all-done.4 = f32[16,24,3584]{2,1,0:T(8,128)} async-done(((f32[16,24,3584]{2,1,0:T(8,128)}), f32[16,24,3584]{2,1,0:T(8,128)}, u32[]{:S(2)}, u32[]{:S(2)}) %all-to-all-start.4) | async-done | bytes 5505056 | tf_op jit(solution)/shard_map/all_to_all | solution.py:36
  333.0 4.5 %gather_fusion.2 = f32[128,3584]{1,0:T(8,128)} fusion(f32[16,24,3584]{2,1,0:T(8,128)} %all-to-all-done.4, s32[128]{0:T(128)S(1)} %get-tuple-element.27), kind=kCustom, calls=%fused_computation.2 | custom fusion | bytes 3671040 | tf_op jit(solution)/shard_map/gather | solution.py:98
  337.6 2.7 copy.145
  340.3 3.6 fusion.10
  343.9 2.6 copy.148
  346.5 3.3 convert_element_type.22
  349.8 4.4 %all-to-all-start.5 = ((bf16[2,64,3584]{2,1,0:T(8,128)(2,1)}), bf16[2,64,3584]{2,1,0:T(8,128)(2,1)}, u32[]{:S(2)}, u32[]{:S(2)}) async-start(bf16[2,64,3584]{2,1,0:T(8,128)(2,1)} %convert_element_type.22), calls=%async_computation.5 | async-start | bytes 1835008 | tf_op jit(solution)/shard_map/all_to_all | solution.py:110
  354.2 0.1 slice.36
  354.3 3.1 copy.150
  357.4 9.9 %all-to-all-done.5 = bf16[2,64,3584]{2,1,0:T(8,128)(2,1)} async-done(((bf16[2,64,3584]{2,1,0:T(8,128)(2,1)}), bf16[2,64,3584]{2,1,0:T(8,128)(2,1)}, u32[]{:S(2)}, u32[]{:S(2)}) %all-to-all-start.5) | async-done | bytes 917536 | tf_op jit(solution)/shard_map/all_to_all | solution.py:110
  367.3 2.2 copy.153
  (27 shorter events, 1.2 us)
Async XLA Ops:
  4.4 5.2 %copy-start.3 = (s32[1,8]{1,0:T(1,128)S(1)}, s32[1,8]{1,0:T(1,128)}, u32[]{:S(2)}) copy-start(s32[1,8]{1,0:T(1,128)} %param.7) | copy-start | bytes 100
  4.4 5.5 %copy-start.2 = (s32[1,8]{1,0:T(1,128)S(1)}, s32[1,8]{1,0:T(1,128)}, u32[]{:S(2)}) copy-start(s32[1,8]{1,0:T(1,128)} %param.8) | copy-start | bytes 100
  4.4 5.6 %copy-start.4 = (s32[16]{0:T(128)S(1)}, s32[16]{0:T(128)}, u32[]{:S(2)}) copy-start(s32[16]{0:T(128)} %param.9) | copy-start | bytes 196
  4.4 37.4 %all-to-all-start = ((bf16[2,64,3,3584]{3,1,2,0:T(8,128)(2,1)}), bf16[2,64,3,3584]{3,1,2,0:T(8,128)(2,1)}, u32[]{:S(2)}, u32[]{:S(2)}) async-start(bf16[2,64,3,3584]{3,1,2,0:T(8,128)(2,1)} %pad_maximum_fusion), calls=%async_computation | async-start | bytes 5505024 | tf_op jit(solution)/shard_map/all_to_all | solution.py:44
  80.8 67.7 %all-to-all-start.1 = ((bf16[16,24,3584]{2,1,0:T(8,128)(2,1)}), bf16[16,24,3584]{2,1,0:T(8,128)(2,1)}, u32[]{:S(2)}, u32[]{:S(2)}) async-start(bf16[16,24,3584]{2,1,0:T(8,128)(2,1)} %scatter_fusion), calls=%async_computation.1 | async-start | bytes 5505024 | tf_op jit(solution)/shard_map/all_to_all | solution.py:95
  160.9 2.7 copy-start
  164.5 14.5 %all-to-all-start.2 = ((f32[16,1,384]{2,1,0:T(1,128)}), f32[16,1,384]{2,1,0:T(1,128)S(1)}, u32[]{:S(2)}, u32[]{:S(2)}) async-start(f32[16,1,384]{2,1,0:T(1,128)} %reshape.150), calls=%async_computation.2 | async-start | bytes 49152 | tf_op jit(solution)/shard_map/all_to_all | solution.py:38
  179.0 27.7 %all-to-all-start.3 = ((f32[16,1,384]{2,1,0:T(1,128)}), f32[16,1,384]{2,1,0:T(1,128)S(1)}, u32[]{:S(2)}, u32[]{:S(2)}) async-start(f32[16,1,384]{2,1,0:T(1,128)} %reshape.152), calls=%async_computation.3 | async-start | bytes 49152 | tf_op jit(solution)/shard_map/all_to_all | solution.py:37
  206.7 126.3 %all-to-all-start.4 = ((f32[16,24,3584]{2,1,0:T(8,128)}), f32[16,24,3584]{2,1,0:T(8,128)}, u32[]{:S(2)}, u32[]{:S(2)}) async-start(f32[16,24,3584]{2,1,0:T(8,128)} %reshape.124), calls=%async_computation.4 | async-start | bytes 11010048 | tf_op jit(solution)/shard_map/all_to_all | solution.py:36
  221.5 1.0 copy-start.1
  349.8 17.5 %all-to-all-start.5 = ((bf16[2,64,3584]{2,1,0:T(8,128)(2,1)}), bf16[2,64,3584]{2,1,0:T(8,128)(2,1)}, u32[]{:S(2)}, u32[]{:S(2)}) async-start(bf16[2,64,3584]{2,1,0:T(8,128)(2,1)} %convert_element_type.22), calls=%async_computation.5 | async-start | bytes 1835008 | tf_op jit(solution)/shard_map/all_to_all | solution.py:110
